TPU v7x, 256 devices: a whole 4x4x8 slice. The times are simulated.
256 devices in a mesh: clients: 32 (over z_hi, y, core), fsdp: 8 (over x, z_lo).
Axes of the slice: x: 4, y: 4, z: 8 (z_hi: 4, z_lo: 2; z = z_hi * 2 + z_lo), core: 2. Of those that a mesh axis runs over, the one named last changes fastest.
Arguments:
- token_ids: int32 [32, 5120], P('clients', 'fsdp'), may hold values from 0 to 16383
- target: bfloat16 [32, 5120, 768], P('clients', 'fsdp'), may hold values from -6 to 6
- embedding: bfloat16 [16384, 768], P(None, 'fsdp'), may hold values from -6 to 6
- norm_gain: float32 [768], replicated, may hold values from 0.1 to 1.9
- global_model: float32 [3, 768, 1024], P(None, 'fsdp', 'clients'), may hold values from -0.21875 to 0.21875
- global_control: float32 [3, 768, 1024], P(None, 'fsdp', 'clients'), may hold values from -140 to 140
- client_control: float32 [32, 3, 768, 1024], P('clients', None, 'fsdp'), may hold values from -150 to 150
- local_steps: int32 [32], replicated, may hold values from 1 to 2
- client_weight: int32 [32], replicated, may hold values from 1 to 4
Outputs:
- server_step: float32 [3, 768, 1024], P(None, 'fsdp', 'clients')
- server_control: float32 [3, 768, 1024], P(None, 'fsdp', 'clients')
- client_update: float32 [32, 3, 768, 1024], P('clients', None, 'fsdp')
All inputs are finite; a program needn't handle non-finite values.
Results may differ from a plain program's by a relative error of at most 0.025.
Values may be sent and summed in bfloat16 or wider, within the bound.
No kernel may reach another device: no remote copies, remote signals or barrier semaphores. Data moves between devices by JAX's collectives and lax.ppermute only.
A program may use at most 64 MiB of HBM per device.

v0:
```python
import math
import jax
import jax.numpy as jnp
from jax import lax
from jax.sharding import PartitionSpec as P

LOCAL = 2
learning_rate = 0.005
norm_eps = 1e-06


def copy_for_each(x, axis):
    size = lax.axis_size(axis)
    return lax.all_to_all(jnp.broadcast_to(x[None], (size, *x.shape)), axis, 0, 0, tiled=True)


def joined_along(pieces, dim):
    dims = list(pieces.shape[1:])
    dims[dim] *= pieces.shape[0]
    return jnp.moveaxis(pieces, 0, dim).reshape(dims)


def gathered_copies(x, axis, dim):
    pieces = copy_for_each(x, axis)
    return joined_along(pieces, dim)


def gather_turned(arrays, axis, dims):
    turned = [jnp.moveaxis(a, dim, 0) for a, dim in zip(arrays, dims)]
    widths = [t[0].size for t in turned]
    both = jnp.concatenate([t.reshape(-1, w) for t, w in zip(turned, widths)], axis=1)
    filled = lax.all_gather(both, axis, axis=0, tiled=True)
    pieces = jnp.split(filled, [sum(widths[:k]) for k in range(1, len(widths))], axis=1)
    return tuple(
        (
            jnp.moveaxis(b.reshape(-1, *t.shape[1:]), 0, dim)
            for b, t, dim in zip(pieces, turned, dims)
        )
    )


def cut_along(x, dim, size):
    before, after = (x.shape[:dim], x.shape[dim + 1 :])
    return jnp.moveaxis(x.reshape(*before, size, -1, *after), dim, 0)


def summed_on_arrival(x, axis, dim):
    pieces = cut_along(x, dim, lax.axis_size(axis))
    arrived = lax.all_to_all(pieces, axis, split_axis=0, concat_axis=0, tiled=True)
    return arrived.astype(jnp.float32).sum(axis=0)


def in_one_piece(arrays, axis, dim, along):
    ends, at = ([], 0)
    for a in arrays[:-1]:
        at += a.shape[along]
        ends.append(at)
    both = jnp.concatenate(arrays, axis=along)
    return tuple(
        jnp.split(lax.psum_scatter(both, axis, scatter_dimension=dim, tiled=True), ends, axis=along)
    )


def gelu_pair(pre_act):
    return jax.vjp(lambda inputs: jax.nn.gelu(inputs, approximate=True), pre_act)


def contract_rows(left, right):
    return lax.dot_general(
        left, right, (((0,), (0,)), ((), ())), preferred_element_type=jnp.float32
    )


def body(
    token_ids,
    target,
    embedding,
    norm_gain,
    global_model,
    global_control,
    client_control,
    local_steps,
    client_weight,
):
    tok_rows = target.shape[1]
    group_rows = tok_rows * lax.axis_size("fsdp")
    loss_scale = 1.0 / math.sqrt(group_rows)
    all_ids = gathered_copies(token_ids, "fsdp", 1)
    emb_columns = jnp.take(embedding, all_ids[0], axis=0)
    embedded = lax.all_to_all(emb_columns, "fsdp", split_axis=0, concat_axis=1, tiled=True)
    widened = embedded.astype(jnp.float32)
    inv_norm = lax.rsqrt(jnp.mean(widened * widened, axis=1, keepdims=True) + norm_eps)
    normed = (widened * inv_norm * norm_gain).astype(jnp.bfloat16)
    target_rows = target[0].astype(jnp.float32)
    model_rows, control_rows = tuple(
        (
            part.astype(jnp.float32)
            for part in gather_turned(
                (global_model.astype(jnp.bfloat16), global_control.astype(jnp.bfloat16)),
                "clients",
                (2, 2),
            )
        )
    )
    client_index = lax.axis_index("clients")
    slots = jnp.arange(local_steps.shape[0])
    step_count = jnp.sum(jnp.where(slots == client_index, local_steps, 0))
    own_weight = jnp.sum(jnp.where(slots == client_index, client_weight, 0)).astype(jnp.float32)
    weight_total = jnp.sum(client_weight).astype(jnp.float32)
    correction = control_rows - client_control[0]
    pseudo = jnp.zeros(model_rows.shape, jnp.float32)
    for local_step in range(LOCAL):
        current = (model_rows - learning_rate * pseudo).astype(jnp.bfloat16)
        gathered = lax.all_gather(current, "fsdp", axis=1, tiled=True)
        gate_pre = jnp.dot(normed, gathered[0], preferred_element_type=jnp.float32)
        up_pre = jnp.dot(normed, gathered[1], preferred_element_type=jnp.float32)
        gate_act, gelu_back = gelu_pair(gate_pre)
        hidden = (gate_act * up_pre).astype(jnp.bfloat16)
        projected = lax.dot_general(
            hidden, gathered[2], (((1,), (1,)), ((), ())), preferred_element_type=jnp.float32
        )
        out_grad = ((widened + projected - target_rows) * loss_scale).astype(jnp.bfloat16)
        hidden_grad = jnp.dot(out_grad, gathered[2], preferred_element_type=jnp.float32)
        gate_grad = gelu_back(hidden_grad * up_pre)[0].astype(jnp.bfloat16)
        up_grad = (hidden_grad * gate_act).astype(jnp.bfloat16)
        grad_terms = jnp.stack(
            [
                contract_rows(normed, gate_grad),
                contract_rows(normed, up_grad),
                contract_rows(out_grad, hidden),
            ]
        )
        grads = summed_on_arrival(grad_terms.astype(jnp.bfloat16), "fsdp", 1)
        step_mask = (local_step < step_count).astype(jnp.float32)
        pseudo = pseudo + step_mask * (grads + correction)
    update = client_control[0] - control_rows + pseudo / step_count.astype(jnp.float32)
    step_sum, control_sum = tuple(
        (
            part.astype(jnp.float32)
            for part in in_one_piece(
                (
                    (own_weight * pseudo).astype(jnp.bfloat16),
                    (own_weight * update).astype(jnp.bfloat16),
                ),
                "clients",
                2,
                0,
            )
        )
    )
    return (step_sum / weight_total, control_sum / weight_total, update[None])


def solution(mesh):
    placed = (
        P("clients", "fsdp"),
        P("clients", "fsdp", None),
        P(None, "fsdp"),
        P(),
        P(None, "fsdp", "clients"),
        P(None, "fsdp", "clients"),
        P("clients", None, "fsdp", None),
        P(),
        P(),
    )
    return jax.shard_map(
        body,
        mesh=mesh,
        in_specs=placed,
        out_specs=(
            P(None, "fsdp", "clients"),
            P(None, "fsdp", "clients"),
            P("clients", None, "fsdp", None),
        ),
        check_vma=False,
    )
```

profile of v0, /device:TPU:4, one launch (start us, length us, event | category | flops | bytes accessed | tf_op | source)
XLA Modules:
  0.0 550.3 jit_solution(11312081025137654549)
XLA Ops:
  7.2 0.8 convert_bitcast_fusion.2
  8.1 0.8 convert_bitcast_fusion.1
  9.1 0.7 pad_maximum_fusion.1
  9.8 56.8 %all-gather.4.cloned.1.call-done = bf16[1024,576]{1,0:T(8,128)(2,1)} async-done(((bf16[32,576]{1,0:T(8,128)(2,1)}), bf16[1024,576]{1,0:T(8,128)(2,1)}) %all-gather.4.cloned.1.call-update) | async-done | bytes 1179664 | tf_op jit(solution)/shard_map/all_gather | solution.py:32
  66.7 3.0 fusion.63
  69.6 2.2 copy.80
  71.9 0.6 broadcast_in_dim.30
  72.5 4.8 all-to-all-start
  77.3 3.9 copy.66
  81.3 16.5 %gather_fusion = bf16[5120,96]{1,0:T(8,128)(2,1)S(1)} fusion(bf16[16384,96]{1,0:T(8,128)(2,1)} %copy.66, s32[5120]{0:T(1024)S(1)} %broadcast_clamp_fusion), kind=kCustom, calls=%fused_computation | custom fusion | bytes 1986560 | tf_op jit(solution)/shard_map/jit(_take)/gather | solution.py:89
  97.8 0.7 copy.67
  98.5 1.1 broadcast_select_fusion
  99.6 5.8 %all-to-all-start.1 = ((bf16[8,640,96]{1,2,0:T(8,128)(2,1)}), bf16[8,640,96]{1,2,0:T(8,128)(2,1)S(1)}, u32[]{:S(2)}, u32[]{:S(2)}) async-start(bf16[8,640,96]{1,2,0:T(8,128)(2,1)} %broadcast_select_fusion), calls=%async_computation.1 | async-start | bytes 1966080 | tf_op jit(solution)/shard_map/all_to_all | solution.py:90
  105.4 23.6 %all-to-all-done.1 = bf16[8,640,96]{1,2,0:T(8,128)(2,1)S(1)} async-done(((bf16[8,640,96]{1,2,0:T(8,128)(2,1)}), bf16[8,640,96]{1,2,0:T(8,128)(2,1)S(1)}, u32[]{:S(2)}, u32[]{:S(2)}) %all-to-all-start.1) | async-done | bytes 983072 | tf_op jit(solution)/shard_map/all_to_all | solution.py:90
  129.2 1.8 copy.71
  131.8 50.4 %all-gather.6.cloned.1.call-done = bf16[3,768,1024]{2,1,0:T(8,128)(2,1)} async-done(((bf16[3,96,1024]{2,1,0:T(8,128)(2,1)}), bf16[3,768,1024]{2,1,0:T(8,128)(2,1)}) %all-gather.6.cloned.1.call-update) | async-done | bytes 4718608 | tf_op jit(solution)/shard_map/all_gather | solution.py:114
  182.2 2.8 fusion.21
  185.0 1.8 multiply_convert_fusion.3
  186.8 1.3 fusion.15
  188.1 1.4 convolution_convert_fusion.3
  189.5 1.2 fusion.26
  190.7 1.6 fusion.23
  192.3 2.7 fusion.22
  195.6 2.7 copy.72
  198.3 6.0 %all-to-all-start.2 = ((bf16[8,3,96,1024]{3,2,1,0:T(8,128)(2,1)}), bf16[8,3,96,1024]{3,2,1,0:T(8,128)(2,1)}, u32[]{:S(2)}, u32[]{:S(2)}) async-start(bf16[8,3,96,1024]{3,2,1,0:T(8,128)(2,1)} %copy.72), calls=%async_computation.2 | async-start | bytes 9437184 | tf_op jit(solution)/shard_map/all_to_all | solution.py:49
  204.4 0.6 fusion.40
  205.9 50.9 %all-to-all-done.2 = bf16[8,3,96,1024]{3,2,1,0:T(8,128)(2,1)} async-done(((bf16[8,3,96,1024]{3,2,1,0:T(8,128)(2,1)}), bf16[8,3,96,1024]{3,2,1,0:T(8,128)(2,1)}, u32[]{:S(2)}, u32[]{:S(2)}) %all-to-all-start.2) | async-done | bytes 4718624 | tf_op jit(solution)/shard_map/all_to_all | solution.py:49
  256.9 3.5 convert_reduce_fusion.1
  260.4 1.2 subtract_convert_fusion
  261.6 103.7 %all-gather.8.cloned.1.call-done = bf16[3,768,1024]{2,1,0:T(8,128)(2,1)} async-done(((bf16[3,96,1024]{2,1,0:T(8,128)(2,1)}), bf16[3,768,1024]{2,1,0:T(8,128)(2,1)}) %all-gather.8.cloned.1.call-update) | async-done | bytes 4718608 | tf_op jit(solution)/shard_map/all_gather | solution.py:114
  365.3 3.1 fusion.19
  368.7 1.8 multiply_convert_fusion.1
  370.5 1.3 fusion.17
  371.8 1.4 convolution_convert_fusion
  373.3 1.2 fusion.27
  374.5 1.5 fusion.25
  376.0 2.7 fusion.24
  379.3 2.7 copy.75
  382.1 6.0 %all-to-all-start.3 = ((bf16[8,3,96,1024]{3,2,1,0:T(8,128)(2,1)}), bf16[8,3,96,1024]{3,2,1,0:T(8,128)(2,1)}, u32[]{:S(2)}, u32[]{:S(2)}) async-start(bf16[8,3,96,1024]{3,2,1,0:T(8,128)(2,1)} %copy.75), calls=%async_computation.3 | async-start | bytes 9437184 | tf_op jit(solution)/shard_map/all_to_all | solution.py:49
  389.4 0.6 fusion.61
  390.6 49.9 %all-to-all-done.3 = bf16[8,3,96,1024]{3,2,1,0:T(8,128)(2,1)} async-done(((bf16[8,3,96,1024]{3,2,1,0:T(8,128)(2,1)}), bf16[8,3,96,1024]{3,2,1,0:T(8,128)(2,1)}, u32[]{:S(2)}, u32[]{:S(2)}) %all-to-all-start.3) | async-done | bytes 4718624 | tf_op jit(solution)/shard_map/all_to_all | solution.py:49
  440.6 3.5 convert_reduce_fusion
  444.1 1.6 multiply_convert_fusion.6
  445.8 2.8 copy.76
  449.2 92.3 %reduce-scatter.2.cloned.1.call-done = bf16[6,96,32]{1,0,2:T(8,128)(2,1)} async-done(((bf16[6,96,1024]{1,0,2:T(8,128)(2,1)}), bf16[6,96,32]{1,0,2:T(8,128)(2,1)}) %reduce-scatter.2.cloned.1.call-update) | async-done | bytes 36880 | tf_op jit(solution)/shard_map/reduce_scatter | solution.py:60
  541.5 0.9 convert_divide_fusion
  542.5 0.6 copy.78
  543.1 0.6 copy.77
  (63 shorter events, 3.3 us)
Async XLA Ops:
  7.2 59.5 %all-gather.4.cloned.1.call-start = ((), (), s32[]{:S(2)}) async-start(), calls=%async_computation.5 | async-start | bytes 1351680 | tf_op jit(solution)/shard_map/all_gather | solution.py:32
  9.1 62.8 %copy-start.11 = (s32[1,640]{1,0:T(1,128)S(1)}, s32[1,640]{1,0:T(1,128)}, u32[]{:S(2)}) copy-start(s32[1,640]{1,0:T(1,128)} %param.9) | copy-start | bytes 7684
  9.8 67.6 %copy-start.2 = (bf16[16384,96]{0,1:T(8,128)(2,1)S(1)}, bf16[16384,96]{0,1:T(8,128)(2,1)}, u32[]{:S(2)}) copy-start(bf16[16384,96]{0,1:T(8,128)(2,1)} %param.11) | copy-start | bytes 9437188
  9.8 172.4 %all-gather.6.cloned.1.call-start = ((), (), s32[]{:S(2)}) async-start(), calls=%async_computation.6 | async-start | bytes 5308416 | tf_op jit(solution)/shard_map/all_gather | solution.py:114
  72.5 8.8 %all-to-all-start = ((s32[8,1,640]{2,1,0:T(1,128)}), s32[8,1,640]{2,1,0:T(1,128)S(1)}, u32[]{:S(2)}, u32[]{:S(2)}) async-start(s32[8,1,640]{2,1,0:T(1,128)} %broadcast_in_dim.30), calls=%async_computation | async-start | bytes 40960 | tf_op jit(solution)/shard_map/all_to_all | solution.py:14
  97.8 7.5 %copy-start.10 = (f32[768]{0:T(1024)S(1)}, f32[768]{0:T(1024)}, u32[]{:S(2)}) copy-start(f32[768]{0:T(1024)} %param.12) | copy-start | bytes 9220
  99.6 29.5 %all-to-all-start.1 = ((bf16[8,640,96]{1,2,0:T(8,128)(2,1)}), bf16[8,640,96]{1,2,0:T(8,128)(2,1)S(1)}, u32[]{:S(2)}, u32[]{:S(2)}) async-start(bf16[8,640,96]{1,2,0:T(8,128)(2,1)} %broadcast_select_fusion), calls=%async_computation.1 | async-start | bytes 1966080 | tf_op jit(solution)/shard_map/all_to_all | solution.py:90
  131.5 60.8 %copy-start.6 = (bf16[640,768]{0,1:T(8,128)(2,1)}, bf16[640,768]{0,1:T(8,128)(2,1)S(1)}, u32[]{:S(2)}) copy-start(bf16[640,768]{0,1:T(8,128)(2,1)S(1)} %multiply_convert_fusion.5) | copy-start | bytes 2949124
  131.8 53.2 %copy-start.8 = (bf16[8,640,96]{1,2,0:T(8,128)(2,1)}, bf16[8,640,96]{1,2,0:T(8,128)(2,1)S(1)}, u32[]{:S(2)}) copy-start(bf16[8,640,96]{1,2,0:T(8,128)(2,1)S(1)} %multiply_convert_fusion.4) | copy-start | bytes 2949124
  182.2 2.8 copy-start.13
  185.0 1.8 copy-start.4
  185.0 1.8 copy-start.15
  198.3 6.0 %copy-start.17 = (s32[32]{0:T(128)S(1)}, s32[32]{0:T(128)}, u32[]{:S(2)}) copy-start(s32[32]{0:T(128)} %param.16) | copy-start | bytes 388
  198.3 7.3 %copy-start.3 = (bf16[1024,288]{1,0:T(8,128)(2,1)S(1)}, bf16[1024,288]{1,0:T(8,128)(2,1)}, u32[]{:S(2)}) copy-start(bf16[1024,288]{1,0:T(8,128)(2,1)} %get-tuple-element.26) | copy-start | bytes 1769476
  198.3 58.5 %all-to-all-start.2 = ((bf16[8,3,96,1024]{3,2,1,0:T(8,128)(2,1)}), bf16[8,3,96,1024]{3,2,1,0:T(8,128)(2,1)}, u32[]{:S(2)}, u32[]{:S(2)}) async-start(bf16[8,3,96,1024]{3,2,1,0:T(8,128)(2,1)} %copy.72), calls=%async_computation.2 | async-start | bytes 9437184 | tf_op jit(solution)/shard_map/all_to_all | solution.py:49
  204.3 160.9 %all-gather.8.cloned.1.call-start = ((), (), s32[]{:S(2)}) async-start(), calls=%async_computation.7 | async-start | bytes 5308416 | tf_op jit(solution)/shard_map/all_gather | solution.py:114
  205.9 54.4 %copy-start = (bf16[1024,288]{0,1:T(8,128)(2,1)S(1)}, bf16[1024,288]{0,1:T(8,128)(2,1)}, u32[]{:S(2)}) copy-start(bf16[1024,288]{0,1:T(8,128)(2,1)} %copy.80) | copy-start | bytes 1769476
  205.9 54.4 %copy-start.1 = (f32[1,3,96,1024]{3,2,1,0:T(8,128)S(1)}, f32[1,3,96,1024]{3,2,1,0:T(8,128)}, u32[]{:S(2)}) copy-start(f32[1,3,96,1024]{3,2,1,0:T(8,128)} %param.15) | copy-start | bytes 3538948
  365.3 3.1 copy-start.9
  365.3 3.4 copy-start.14
  368.7 1.8 copy-start.5
  368.7 1.8 copy-start.16
  373.3 1.2 copy-start.7
  382.1 7.3 %copy-start.12 = (s32[32]{0:T(128)S(1)}, s32[32]{0:T(128)}, u32[]{:S(2)}) copy-start(s32[32]{0:T(128)} %param.17) | copy-start | bytes 388
  382.1 58.5 %all-to-all-start.3 = ((bf16[8,3,96,1024]{3,2,1,0:T(8,128)(2,1)}), bf16[8,3,96,1024]{3,2,1,0:T(8,128)(2,1)}, u32[]{:S(2)}, u32[]{:S(2)}) async-start(bf16[8,3,96,1024]{3,2,1,0:T(8,128)(2,1)} %copy.75), calls=%async_computation.3 | async-start | bytes 9437184 | tf_op jit(solution)/shard_map/all_to_all | solution.py:49
  388.0 153.5 %reduce-scatter.2.cloned.1.call-start = ((), (), s32[]{:S(2)}) async-start(), calls=%async_computation.8 | async-start | bytes 2162688 | tf_op jit(solution)/shard_map/reduce_scatter | solution.py:60
Sparse Core Ops, SparseCore 0:
  11.1 55.5 all-gather.3
  72.0 110.1 all-gather.5
  261.7 103.5 all-gather.7
  448.7 92.7 reduce-scatter.1
where the time goes:
time: 551 us; the launch traced here: 550 us
  waiting for transfers between devices  428 us (78%)
  local copies, waits for them, and re-layouts  39.2 us (7%)
  matrix products  25.7 us (5%)
  starting transfers between devices  22.6 us (4%)
  other arithmetic  17.6 us (3%)
  between operations  17.4 us (3%)
    all_gather x2, waiting for transfers between devices, body(): gathered = lax.all_gather(current, 'fsdp', axis=1, tiled=True)  154 us
    all_to_all x2, waiting for transfers between devices, summed_on_arrival(): lax.all_to_all(pieces, axis, split_axis=0, concat_axis=0, tiled=True)  101 us
    reduce_scatter x1, waiting for transfers between devices, in_one_piece(): lax.psum_scatter(both, axis, scatter_dimension=dim, tiled=True)  92.3 us
    all_gather x1, waiting for transfers between devices, gather_turned(): filled = lax.all_gather(both, axis, axis=0, tiled=True)  56.8 us
    all_to_all x1, waiting for transfers between devices, body(): lax.all_to_all(emb_columns, 'fsdp', split_axis=0, concat_axis=1, tiled=True)  23.6 us
    gather x2, local copies, waits for them, and re-layouts, body(): emb_columns = jnp.take(embedding, all_ids[0], axis=0)  17.1 us
    all_to_all x2, starting transfers between devices, summed_on_arrival(): lax.all_to_all(pieces, axis, split_axis=0, concat_axis=0, tiled=True)  12 us
    dot_general x6, matrix products, contract_rows(): lax.dot_general(left, right, (((0,), (0,)), ((), ())), preferred_element_...  11.4 us
  transfers between devices with their start and end apart: 8, of which 7 were waited for; matrix products, arithmetic and copies ran while one was open for 5% of the time, Pallas kernels for 0%

commit v1 on v0

--- a/solution.py
+++ b/solution.py
@@ -87,7 +87,9 @@
     loss_scale = 1.0 / math.sqrt(group_rows)
     all_ids = gathered_copies(token_ids, "fsdp", 1)
     emb_columns = jnp.take(embedding, all_ids[0], axis=0)
-    embedded = lax.all_to_all(emb_columns, "fsdp", split_axis=0, concat_axis=1, tiled=True)
+    cells = jnp.split(emb_columns, lax.axis_size("fsdp"), axis=0)
+    received = lax.all_to_all(jnp.stack(cells), "fsdp", 0, 0)
+    embedded = jnp.concatenate(received, axis=1)
     widened = embedded.astype(jnp.float32)
     inv_norm = lax.rsqrt(jnp.mean(widened * widened, axis=1, keepdims=True) + norm_eps)
     normed = (widened * inv_norm * norm_gain).astype(jnp.bfloat16)

time: 551 us -> 551 us (level)
    gather x2 -> x1, local copies, waits for them, and re-layouts: 17.1 us -> 16.5 us  [body(): emb_columns = jnp.take(embedding, all_ids[0], axis=0)]
where the time goes in v1:
time: 551 us; the launch traced here: 550 us
  waiting for transfers between devices  425 us (77%)
  local copies, waits for them, and re-layouts  40.1 us (7%)
  matrix products  25.7 us (5%)
  starting transfers between devices  22.6 us (4%)
  other arithmetic  19.2 us (3%)
  between operations  17.4 us (3%)
    all_gather x2, waiting for transfers between devices, body(): gathered = lax.all_gather(current, 'fsdp', axis=1, tiled=True)  152 us
    all_to_all x2, waiting for transfers between devices, summed_on_arrival(): lax.all_to_all(pieces, axis, split_axis=0, concat_axis=0, tiled=True)  101 us
    reduce_scatter x1, waiting for transfers between devices, in_one_piece(): lax.psum_scatter(both, axis, scatter_dimension=dim, tiled=True)  92.3 us
    all_gather x1, waiting for transfers between devices, gather_turned(): filled = lax.all_gather(both, axis, axis=0, tiled=True)  56.8 us
    all_to_all x1, waiting for transfers between devices, body(): received = lax.all_to_all(jnp.stack(cells), 'fsdp', 0, 0)  23.6 us
    gather x1, local copies, waits for them, and re-layouts, body(): emb_columns = jnp.take(embedding, all_ids[0], axis=0)  16.5 us
    all_to_all x2, starting transfers between devices, summed_on_arrival(): lax.all_to_all(pieces, axis, split_axis=0, concat_axis=0, tiled=True)  12 us
    dot_general x6, matrix products, contract_rows(): lax.dot_general(left, right, (((0,), (0,)), ((), ())), preferred_element_...  11.4 us
  transfers between devices with their start and end apart: 8, of which 7 were waited for; matrix products, arithmetic and copies ran while one was open for 5% of the time, Pallas kernels for 0%

profile of v1, /device:TPU:4, one launch (start us, length us, event | category | flops | bytes accessed | tf_op | source)
XLA Modules:
  0.0 550.3 jit_solution(8721858508441281512)
XLA Ops:
  7.2 0.8 convert_bitcast_fusion.2
  8.1 0.8 convert_bitcast_fusion.1
  9.1 0.7 pad_maximum_fusion.1
  9.8 56.8 %all-gather.4.cloned.1.call-done = bf16[1024,576]{1,0:T(8,128)(2,1)} async-done(((bf16[32,576]{1,0:T(8,128)(2,1)}), bf16[1024,576]{1,0:T(8,128)(2,1)}) %all-gather.4.cloned.1.call-update) | async-done | bytes 1179664 | tf_op jit(solution)/shard_map/all_gather | solution.py:32
  66.7 3.0 fusion.71
  69.6 2.2 copy.81
  71.9 0.6 broadcast_in_dim.30
  72.5 4.8 all-to-all-start
  77.3 3.9 copy.68
  81.3 16.5 %gather_fusion = bf16[5120,96]{1,0:T(8,128)(2,1)S(1)} fusion(bf16[16384,96]{1,0:T(8,128)(2,1)} %copy.68, s32[5120]{0:T(1024)S(1)} %broadcast_clamp_fusion), kind=kCustom, calls=%fused_computation | custom fusion | bytes 1986560 | tf_op jit(solution)/shard_map/jit(_take)/gather | solution.py:89
  97.8 2.7 broadcast_select_fusion
  100.7 1.4 copy.69
  102.1 5.8 %all-to-all-start.1 = ((bf16[8,640,96]{1,2,0:T(8,128)(2,1)}), bf16[8,640,96]{1,2,0:T(8,128)(2,1)S(1)}, u32[]{:S(2)}, u32[]{:S(2)}) async-start(bf16[8,640,96]{1,2,0:T(8,128)(2,1)} %copy.69), calls=%async_computation.1 | async-start | bytes 1966080 | tf_op jit(solution)/shard_map/all_to_all | solution.py:91
  107.9 23.6 %all-to-all-done.1 = bf16[8,640,96]{1,2,0:T(8,128)(2,1)S(1)} async-done(((bf16[8,640,96]{1,2,0:T(8,128)(2,1)}), bf16[8,640,96]{1,2,0:T(8,128)(2,1)S(1)}, u32[]{:S(2)}, u32[]{:S(2)}) %all-to-all-start.1) | async-done | bytes 983072 | tf_op jit(solution)/shard_map/all_to_all | solution.py:91
  131.7 1.8 copy.73
  134.4 47.8 %all-gather.6.cloned.1.call-done = bf16[3,768,1024]{2,1,0:T(8,128)(2,1)} async-done(((bf16[3,96,1024]{2,1,0:T(8,128)(2,1)}), bf16[3,768,1024]{2,1,0:T(8,128)(2,1)}) %all-gather.6.cloned.1.call-update) | async-done | bytes 4718608 | tf_op jit(solution)/shard_map/all_gather | solution.py:116
  182.2 2.8 fusion.21
  185.0 1.8 multiply_convert_fusion.3
  186.8 1.3 fusion.15
  188.1 1.4 convolution_convert_fusion.3
  189.5 1.2 fusion.26
  190.7 1.6 fusion.23
  192.3 2.7 fusion.22
  195.6 2.7 copy.74
  198.3 6.0 %all-to-all-start.2 = ((bf16[8,3,96,1024]{3,2,1,0:T(8,128)(2,1)}), bf16[8,3,96,1024]{3,2,1,0:T(8,128)(2,1)}, u32[]{:S(2)}, u32[]{:S(2)}) async-start(bf16[8,3,96,1024]{3,2,1,0:T(8,128)(2,1)} %copy.74), calls=%async_computation.2 | async-start | bytes 9437184 | tf_op jit(solution)/shard_map/all_to_all | solution.py:49
  204.4 0.6 fusion.48
  205.9 50.9 %all-to-all-done.2 = bf16[8,3,96,1024]{3,2,1,0:T(8,128)(2,1)} async-done(((bf16[8,3,96,1024]{3,2,1,0:T(8,128)(2,1)}), bf16[8,3,96,1024]{3,2,1,0:T(8,128)(2,1)}, u32[]{:S(2)}, u32[]{:S(2)}) %all-to-all-start.2) | async-done | bytes 4718624 | tf_op jit(solution)/shard_map/all_to_all | solution.py:49
  256.9 3.5 convert_reduce_fusion.1
  260.4 1.2 subtract_convert_fusion
  261.6 103.7 %all-gather.8.cloned.1.call-done = bf16[3,768,1024]{2,1,0:T(8,128)(2,1)} async-done(((bf16[3,96,1024]{2,1,0:T(8,128)(2,1)}), bf16[3,768,1024]{2,1,0:T(8,128)(2,1)}) %all-gather.8.cloned.1.call-update) | async-done | bytes 4718608 | tf_op jit(solution)/shard_map/all_gather | solution.py:116
  365.3 3.1 fusion.19
  368.7 1.8 multiply_convert_fusion.1
  370.5 1.3 fusion.17
  371.8 1.4 convolution_convert_fusion
  373.3 1.2 fusion.27
  374.5 1.5 fusion.25
  376.0 2.7 fusion.24
  379.3 2.7 copy.77
  382.1 6.0 %all-to-all-start.3 = ((bf16[8,3,96,1024]{3,2,1,0:T(8,128)(2,1)}), bf16[8,3,96,1024]{3,2,1,0:T(8,128)(2,1)}, u32[]{:S(2)}, u32[]{:S(2)}) async-start(bf16[8,3,96,1024]{3,2,1,0:T(8,128)(2,1)} %copy.77), calls=%async_computation.3 | async-start | bytes 9437184 | tf_op jit(solution)/shard_map/all_to_all | solution.py:49
  389.4 0.6 fusion.69
  390.6 49.9 %all-to-all-done.3 = bf16[8,3,96,1024]{3,2,1,0:T(8,128)(2,1)} async-done(((bf16[8,3,96,1024]{3,2,1,0:T(8,128)(2,1)}), bf16[8,3,96,1024]{3,2,1,0:T(8,128)(2,1)}, u32[]{:S(2)}, u32[]{:S(2)}) %all-to-all-start.3) | async-done | bytes 4718624 | tf_op jit(solution)/shard_map/all_to_all | solution.py:49
  440.6 3.5 convert_reduce_fusion
  444.1 1.6 multiply_convert_fusion.6
  445.8 2.8 copy.78
  449.2 92.3 %reduce-scatter.2.cloned.1.call-done = bf16[6,96,32]{1,0,2:T(8,128)(2,1)} async-done(((bf16[6,96,1024]{1,0,2:T(8,128)(2,1)}), bf16[6,96,32]{1,0,2:T(8,128)(2,1)}) %reduce-scatter.2.cloned.1.call-update) | async-done | bytes 36880 | tf_op jit(solution)/shard_map/reduce_scatter | solution.py:60
  541.5 0.9 convert_divide_fusion
  542.5 0.6 copy.80
  543.1 0.6 copy.79
  (71 shorter events, 3.5 us)
Async XLA Ops:
  7.2 59.5 %all-gather.4.cloned.1.call-start = ((), (), s32[]{:S(2)}) async-start(), calls=%async_computation.5 | async-start | bytes 1351680 | tf_op jit(solution)/shard_map/all_gather | solution.py:32
  9.1 62.8 %copy-start.11 = (s32[1,640]{1,0:T(1,128)S(1)}, s32[1,640]{1,0:T(1,128)}, u32[]{:S(2)}) copy-start(s32[1,640]{1,0:T(1,128)} %param.9) | copy-start | bytes 7684
  9.8 67.6 %copy-start.2 = (bf16[16384,96]{0,1:T(8,128)(2,1)S(1)}, bf16[16384,96]{0,1:T(8,128)(2,1)}, u32[]{:S(2)}) copy-start(bf16[16384,96]{0,1:T(8,128)(2,1)} %param.11) | copy-start | bytes 9437188
  9.8 172.4 %all-gather.6.cloned.1.call-start = ((), (), s32[]{:S(2)}) async-start(), calls=%async_computation.6 | async-start | bytes 5308416 | tf_op jit(solution)/shard_map/all_gather | solution.py:116
  72.5 8.8 %all-to-all-start = ((s32[8,1,640]{2,1,0:T(1,128)}), s32[8,1,640]{2,1,0:T(1,128)S(1)}, u32[]{:S(2)}, u32[]{:S(2)}) async-start(s32[8,1,640]{2,1,0:T(1,128)} %broadcast_in_dim.30), calls=%async_computation | async-start | bytes 40960 | tf_op jit(solution)/shard_map/all_to_all | solution.py:14
  100.6 7.2 %copy-start.10 = (f32[768]{0:T(1024)S(1)}, f32[768]{0:T(1024)}, u32[]{:S(2)}) copy-start(f32[768]{0:T(1024)} %param.12) | copy-start | bytes 9220
  102.1 29.5 %all-to-all-start.1 = ((bf16[8,640,96]{1,2,0:T(8,128)(2,1)}), bf16[8,640,96]{1,2,0:T(8,128)(2,1)S(1)}, u32[]{:S(2)}, u32[]{:S(2)}) async-start(bf16[8,640,96]{1,2,0:T(8,128)(2,1)} %copy.69), calls=%async_computation.1 | async-start | bytes 1966080 | tf_op jit(solution)/shard_map/all_to_all | solution.py:91
  134.1 58.2 %copy-start.6 = (bf16[640,768]{0,1:T(8,128)(2,1)}, bf16[640,768]{0,1:T(8,128)(2,1)S(1)}, u32[]{:S(2)}) copy-start(bf16[640,768]{0,1:T(8,128)(2,1)S(1)} %multiply_convert_fusion.5) | copy-start | bytes 2949124
  134.4 50.6 %copy-start.8 = (bf16[8,640,96]{1,2,0:T(8,128)(2,1)}, bf16[8,640,96]{1,2,0:T(8,128)(2,1)S(1)}, u32[]{:S(2)}) copy-start(bf16[8,640,96]{1,2,0:T(8,128)(2,1)S(1)} %multiply_convert_fusion.4) | copy-start | bytes 2949124
  182.2 2.8 copy-start.13
  185.0 1.8 copy-start.4
  185.0 1.8 copy-start.15
  198.3 6.0 %copy-start.17 = (s32[32]{0:T(128)S(1)}, s32[32]{0:T(128)}, u32[]{:S(2)}) copy-start(s32[32]{0:T(128)} %param.16) | copy-start | bytes 388
  198.3 7.3 %copy-start.3 = (bf16[1024,288]{1,0:T(8,128)(2,1)S(1)}, bf16[1024,288]{1,0:T(8,128)(2,1)}, u32[]{:S(2)}) copy-start(bf16[1024,288]{1,0:T(8,128)(2,1)} %get-tuple-element.26) | copy-start | bytes 1769476
  198.3 58.5 %all-to-all-start.2 = ((bf16[8,3,96,1024]{3,2,1,0:T(8,128)(2,1)}), bf16[8,3,96,1024]{3,2,1,0:T(8,128)(2,1)}, u32[]{:S(2)}, u32[]{:S(2)}) async-start(bf16[8,3,96,1024]{3,2,1,0:T(8,128)(2,1)} %copy.74), calls=%async_computation.2 | async-start | bytes 9437184 | tf_op jit(solution)/shard_map/all_to_all | solution.py:49
  204.3 160.9 %all-gather.8.cloned.1.call-start = ((), (), s32[]{:S(2)}) async-start(), calls=%async_computation.7 | async-start | bytes 5308416 | tf_op jit(solution)/shard_map/all_gather | solution.py:116
  205.9 54.4 %copy-start = (bf16[1024,288]{0,1:T(8,128)(2,1)S(1)}, bf16[1024,288]{0,1:T(8,128)(2,1)}, u32[]{:S(2)}) copy-start(bf16[1024,288]{0,1:T(8,128)(2,1)} %copy.81) | copy-start | bytes 1769476
  205.9 54.4 %copy-start.1 = (f32[1,3,96,1024]{3,2,1,0:T(8,128)S(1)}, f32[1,3,96,1024]{3,2,1,0:T(8,128)}, u32[]{:S(2)}) copy-start(f32[1,3,96,1024]{3,2,1,0:T(8,128)} %param.15) | copy-start | bytes 3538948
  365.3 3.1 copy-start.9
  365.3 3.4 copy-start.14
  368.7 1.8 copy-start.5
  368.7 1.8 copy-start.16
  373.3 1.2 copy-start.7
  382.1 7.3 %copy-start.12 = (s32[32]{0:T(128)S(1)}, s32[32]{0:T(128)}, u32[]{:S(2)}) copy-start(s32[32]{0:T(128)} %param.17) | copy-start | bytes 388
  382.1 58.5 %all-to-all-start.3 = ((bf16[8,3,96,1024]{3,2,1,0:T(8,128)(2,1)}), bf16[8,3,96,1024]{3,2,1,0:T(8,128)(2,1)}, u32[]{:S(2)}, u32[]{:S(2)}) async-start(bf16[8,3,96,1024]{3,2,1,0:T(8,128)(2,1)} %copy.77), calls=%async_computation.3 | async-start | bytes 9437184 | tf_op jit(solution)/shard_map/all_to_all | solution.py:49
  388.0 153.5 %reduce-scatter.2.cloned.1.call-start = ((), (), s32[]{:S(2)}) async-start(), calls=%async_computation.8 | async-start | bytes 2162688 | tf_op jit(solution)/shard_map/reduce_scatter | solution.py:60
Sparse Core Ops, SparseCore 0:
  11.1 55.5 all-gather.3
  72.0 110.1 all-gather.5
  261.7 103.5 all-gather.7
  448.7 92.7 reduce-scatter.1
